TPU v7x, 256 devices: a whole 4x4x8 slice. The times are simulated.
256 devices in a mesh: seq: 32 (over y, z), ch: 8 (over x, core).
Axes of the slice: x: 4, y: 4, z: 8, core: 2. Of those that a mesh axis runs over, the one named last changes fastest.
Arguments:
- genome: int32 [8192, 128], P('seq'), may hold values from 0 to 3
- stem_weight: bfloat16 [768, 512], P('ch'), may hold values from -0.5 to 0.5
- dilated_filter_weight: bfloat16 [5, 3, 768, 768], P(None, None, 'ch'), may hold values from -0.125 to 0.125
- head_weight: bfloat16 [768, 5313], P('ch'), may hold values from -0.21875 to 0.21875
- window_start: int32 [512], replicated, may hold values from 0 to 8176
- window_track: int32 [512], replicated, may hold values from 0 to 5312
- targets: float32 [512], replicated, may hold values from 0 to 3
Outputs:
- window_score: float32 [512], replicated
- conv_grad: float32 [5, 3, 768, 768], P(None, None, 'ch', 'seq')
- stem_grad: float32 [768, 512], P('ch')
- head_grad: float32 [768, 5313], P('ch')
Inputs may be any that keep to these rules, and one draw needn't show every extreme that they name: `window_start`: each window lies inside the sequence.
All inputs are finite; a program needn't handle non-finite values.
Results may differ from a plain program's by a relative error of at most 0.0037.
Values may be sent and summed in bfloat16 or wider, within the bound.
A program may use at most 128 MiB of HBM per device.

v0:
```python
import jax
import jax.numpy as jnp
from jax import lax
from jax.sharding import PartitionSpec as P

LAYERS = 5
WIN = 16


def extended(block, sides, width):
    for axis, dim in sides:
        count = lax.axis_size(axis)
        forward = [(i, i + 1) for i in range(count - 1)]
        backward = [(target, source) for source, target in forward]
        low = lax.ppermute(
            lax.slice_in_dim(block, block.shape[dim] - width, None, axis=dim), axis, forward
        )
        high = lax.ppermute(lax.slice_in_dim(block, 0, width, axis=dim), axis, backward)
        block = jnp.concatenate([low, block, high], axis=dim)
    return block


def passed_along(value, axis, by):
    count = lax.axis_size(axis)
    pairs = [(i, i + by) for i in range(count) if 0 <= i + by < count]
    return lax.ppermute(value, axis, pairs)


def dilations(shard_rows):
    return (shard_rows // 8, shard_rows // 2, shard_rows, 2 * shard_rows, 4 * shard_rows)


def reach_rows(field, distance):
    shard_rows = field.shape[2]
    if distance < shard_rows:
        padded = extended(field, (("seq", 2),), distance)
        return (padded[:, :, :shard_rows], padded[:, :, 2 * distance :])
    hop_count = distance // shard_rows
    lower_rows = passed_along(field, "seq", hop_count)
    upper_rows = passed_along(field, "seq", -hop_count)
    return (lower_rows, upper_rows)


def order_taps(lower_rows, middle, upper_rows):
    forward_taps = jnp.stack([lower_rows[0], middle[0], upper_rows[0]])
    reverse_taps = jnp.stack([upper_rows[1], middle[1], lower_rows[1]])
    return jnp.stack([forward_taps, reverse_taps])


def shards(
    genome, stem_weight, dilated_filter_weight, head_weight, window_start, window_track, targets
):
    shard_rows = genome.shape[0]
    spans = dilations(shard_rows)
    letters = (
        (genome[:, :, None] == jnp.arange(4, dtype=jnp.int32))
        .astype(jnp.bfloat16)
        .reshape(shard_rows, -1)
    )
    strands = jnp.stack([letters, letters[:, ::-1]])
    residual_state = jnp.einsum(
        "sri,ci->scr", strands, stem_weight, preferred_element_type=jnp.float32
    )
    saved_states = []
    stored_taps = []
    for current_layer_index in range(LAYERS):
        active = jax.nn.gelu(residual_state).astype(jnp.bfloat16)
        lower_rows, upper_rows = reach_rows(active, spans[current_layer_index])
        resident_taps = order_taps(lower_rows, active, upper_rows)
        collected_taps = lax.all_gather(resident_taps, "ch", axis=2, tiled=True)
        saved_states.append(residual_state)
        stored_taps.append(collected_taps)
        residual_state = residual_state + jnp.einsum(
            "nezp,efz->nfp",
            collected_taps,
            dilated_filter_weight[current_layer_index],
            preferred_element_type=jnp.float32,
        )
    strand_total = residual_state[0] + residual_state[1]
    first_bin = lax.axis_index("seq") * shard_rows
    positions = first_bin + jnp.arange(shard_rows, dtype=jnp.int32)
    member = (
        (positions[None, :] >= window_start[:, None])
        & (positions[None, :] < window_start[:, None] + WIN)
    ).astype(jnp.float32)
    pooled = jnp.einsum("cr,kr->ck", strand_total, member, precision=lax.Precision.HIGHEST) / WIN
    columns = jnp.take(head_weight, window_track, axis=1).astype(jnp.float32)
    partial_score = 0.5 * jnp.sum(pooled * columns, axis=0)
    window_score = lax.psum(partial_score, ("seq", "ch"))
    counts = jnp.sum((window_track[:, None] == window_track[None, :]).astype(jnp.float32), axis=1)
    loss_slope = (jnp.exp(window_score) - targets) / counts
    window_terms = 0.5 * loss_slope[None, :] * pooled
    weights_back = 0.5 / WIN * loss_slope[None, :] * columns
    back_total = jnp.einsum("ck,kr->cr", weights_back, member, precision=lax.Precision.HIGHEST)
    grad_state = jnp.stack([back_total, back_total])
    layer_gradient_list = []
    for current_layer_index in reversed(range(LAYERS)):
        incoming_gradient = grad_state.astype(jnp.bfloat16)
        weight_part = jnp.einsum(
            "pygj,pij->yig",
            stored_taps[current_layer_index],
            incoming_gradient,
            preferred_element_type=jnp.float32,
        )
        layer_gradient_list.append(
            lax.psum_scatter(weight_part, "seq", scatter_dimension=2, tiled=True)
        )
        lower_rows, upper_rows = reach_rows(incoming_gradient, spans[current_layer_index])
        back_taps = order_taps(upper_rows, incoming_gradient, lower_rows)
        spread = jnp.einsum(
            "skor,koc->scr",
            back_taps,
            dilated_filter_weight[current_layer_index],
            preferred_element_type=jnp.float32,
        )
        through = lax.psum_scatter(spread, "ch", scatter_dimension=1, tiled=True)
        pullback = jax.vjp(jax.nn.gelu, saved_states[current_layer_index])[1]
        grad_state = grad_state + pullback(through)[0]
    conv_grad = jnp.stack(layer_gradient_list[::-1])
    stem_part = jnp.einsum(
        "sri,scr->ci", strands, grad_state.astype(jnp.bfloat16), preferred_element_type=jnp.float32
    )
    head_part = jnp.zeros(head_weight.shape, jnp.float32).at[:, window_track].add(window_terms)
    head_grad, stem_grad = lax.psum((head_part, stem_part), "seq")
    return (window_score, conv_grad, stem_grad, head_grad)


def solution(mesh):
    return jax.shard_map(
        shards,
        mesh=mesh,
        in_specs=(
            P("seq", None),
            P("ch", None),
            P(None, None, "ch", None),
            P("ch", None),
            P(),
            P(),
            P(),
        ),
        out_specs=(P(), P(None, None, "ch", "seq"), P("ch", None), P("ch", None)),
        check_vma=False,
    )
```

profile of v0, /device:TPU:1, one launch (start us, length us, event | category | flops | bytes accessed | tf_op | source)
XLA Modules:
  0.0 820.2 jit_solution(104383886669573757)
XLA Ops:
  10.7 4.5 collective-permute-start
  16.5 3.7 collective-permute-done.1
  21.2 32.7 %all-gather.6.cloned.1.call-done = bf16[2,3,768,256]{3,2,1,0:T(8,128)(2,1)} async-done(((bf16[2,3,96,256]{3,2,1,0:T(8,128)(2,1)}), bf16[2,3,768,256]{3,2,1,0:T(8,128)(2,1)}) %all-gather.6.cloned.1.call-update) | async-done | bytes 2359312 | tf_op jit(solution)/shard_map/all_gather | solution.py:70
  53.9 2.2 multiply_convert_fusion.3
  56.1 3.2 collective-permute-start.2
  60.7 3.5 collective-permute-done.3
  65.0 30.5 %all-gather.8.cloned.1.call-done = bf16[2,3,768,256]{3,2,1,0:T(8,128)(2,1)} async-done(((bf16[2,3,96,256]{3,2,1,0:T(8,128)(2,1)}), bf16[2,3,768,256]{3,2,1,0:T(8,128)(2,1)}) %all-gather.8.cloned.1.call-update) | async-done | bytes 2359312 | tf_op jit(solution)/shard_map/all_gather | solution.py:70
  95.5 2.2 multiply_convert_fusion.2
  97.7 3.2 collective-permute-start.4
  102.8 3.8 collective-permute-done.5
  107.5 30.2 %all-gather.10.cloned.1.call-done = bf16[2,3,768,256]{3,2,1,0:T(8,128)(2,1)} async-done(((bf16[2,3,96,256]{3,2,1,0:T(8,128)(2,1)}), bf16[2,3,768,256]{3,2,1,0:T(8,128)(2,1)}) %all-gather.10.cloned.1.call-update) | async-done | bytes 2359312 | tf_op jit(solution)/shard_map/all_gather | solution.py:70
  137.6 2.2 multiply_convert_fusion.1
  139.9 4.2 collective-permute-start.6
  145.9 8.8 %collective-permute-done.7 = bf16[2,96,256]{2,1,0:T(8,128)(2,1)S(1)} collective-permute-done((bf16[2,96,256]{2,1,0:T(8,128)(2,1)S(1)}, bf16[2,96,256]{2,1,0:T(8,128)(2,1)S(1)}, u32[]{:S(2)}, u32[]{:S(2)}) %collective-permute-start.7) | collective-permute-done | bytes 98336 | tf_op jit(solution)/shard_map/ppermute | solution.py:26
  155.6 27.2 %all-gather.12.cloned.1.call-done = bf16[2,3,768,256]{3,2,1,0:T(8,128)(2,1)} async-done(((bf16[2,3,96,256]{3,2,1,0:T(8,128)(2,1)}), bf16[2,3,768,256]{3,2,1,0:T(8,128)(2,1)}) %all-gather.12.cloned.1.call-update) | async-done | bytes 2359312 | tf_op jit(solution)/shard_map/all_gather | solution.py:70
  182.8 2.2 multiply_convert_fusion
  185.0 7.4 collective-permute-start.8
  194.2 8.6 %collective-permute-done.9 = bf16[2,96,256]{2,1,0:T(8,128)(2,1)S(1)} collective-permute-done((bf16[2,96,256]{2,1,0:T(8,128)(2,1)S(1)}, bf16[2,96,256]{2,1,0:T(8,128)(2,1)S(1)}, u32[]{:S(2)}, u32[]{:S(2)}) %collective-permute-start.9) | collective-permute-done | bytes 98336 | tf_op jit(solution)/shard_map/ppermute | solution.py:26
  203.6 2.4 copy.74
  206.1 2.6 gather_fusion
  209.1 22.5 %all-gather.14.cloned.1.call-done = bf16[2,3,768,256]{3,2,1,0:T(8,128)(2,1)} async-done(((bf16[2,3,96,256]{3,2,1,0:T(8,128)(2,1)}), bf16[2,3,768,256]{3,2,1,0:T(8,128)(2,1)}) %all-gather.14.cloned.1.call-update) | async-done | bytes 2359312 | tf_op jit(solution)/shard_map/all_gather | solution.py:70
  231.6 2.2 fusion.6
  235.0 76.7 %psum.21 = f32[512]{0:T(512)S(1)} all-reduce(f32[512]{0:T(512)S(1)} %broadcast_multiply_fusion), channel_id=1, replica_groups=mesh['seq'=32,'ch'=8] {'seq','ch'}, use_global_device_ids=true, to_apply=%region_1.2 | all-reduce | flops 512 | bytes 4096 | tf_op jit(solution)/shard_map/psum | solution.py:89
  313.5 7.9 collective-permute-start.11
  321.6 4.9 collective-permute-done.11
  326.5 1.8 convolution_bitcast_fusion.4
  328.3 32.8 %reduce-scatter.6.cloned.1.call-done = f32[2,96,256]{2,1,0:T(8,128)} async-done(((f32[2,768,256]{2,1,0:T(8,128)}), f32[2,96,256]{2,1,0:T(8,128)}) %reduce-scatter.6.cloned.1.call-update) | async-done | bytes 196624 | tf_op jit(solution)/shard_map/reduce_scatter | solution.py:116
  363.6 4.9 collective-permute-start.13
  370.1 1.8 convolution_bitcast_fusion.3
  372.0 39.8 %reduce-scatter.8.cloned.1.call-done = f32[2,96,256]{2,1,0:T(8,128)} async-done(((f32[2,768,256]{2,1,0:T(8,128)}), f32[2,96,256]{2,1,0:T(8,128)}) %reduce-scatter.8.cloned.1.call-update) | async-done | bytes 196624 | tf_op jit(solution)/shard_map/reduce_scatter | solution.py:116
  414.2 4.0 collective-permute-start.15
  419.9 1.8 convolution_bitcast_fusion.2
  421.7 37.6 %reduce-scatter.10.cloned.1.call-done = f32[2,96,256]{2,1,0:T(8,128)} async-done(((f32[2,768,256]{2,1,0:T(8,128)}), f32[2,96,256]{2,1,0:T(8,128)}) %reduce-scatter.10.cloned.1.call-update) | async-done | bytes 196624 | tf_op jit(solution)/shard_map/reduce_scatter | solution.py:116
  461.7 4.0 collective-permute-start.17
  466.9 1.8 convolution_bitcast_fusion.1
  468.7 37.7 %reduce-scatter.12.cloned.1.call-done = f32[2,96,256]{2,1,0:T(8,128)} async-done(((f32[2,768,256]{2,1,0:T(8,128)}), f32[2,96,256]{2,1,0:T(8,128)}) %reduce-scatter.12.cloned.1.call-update) | async-done | bytes 196624 | tf_op jit(solution)/shard_map/reduce_scatter | solution.py:116
  506.4 1.8 fusion.169
  509.5 4.2 collective-permute-start.19
  514.8 2.9 convolution_bitcast_fusion
  519.6 1.6 copy.89
  521.2 4.4 scatter_custom_fusion
  525.5 2.6 convolution_bitcast_fusion.6
  532.1 2.7 convolution_bitcast_fusion.8
  534.8 1.5 copy.83
  538.7 16.7 %reduce-scatter.14.cloned.1.call-done = f32[2,96,256]{2,1,0:T(8,128)} async-done(((f32[2,768,256]{2,1,0:T(8,128)}), f32[2,96,256]{2,1,0:T(8,128)}) %reduce-scatter.14.cloned.1.call-update) | async-done | bytes 196624 | tf_op jit(solution)/shard_map/reduce_scatter | solution.py:116
  555.5 1.9 convolution_bitcast_fusion.15
  559.3 246.3 %all-reduce.8.cloned.1.call-done = (f32[3,96,768]{1,0,2:T(4,128)}, f32[3,96,768]{1,0,2:T(4,128)}, f32[3,96,768]{1,0,2:T(4,128)}, f32[3,96,768]{1,0,2:T(4,128)}, ...) async-done(((f32[3,96,768]{1,0,2:T(4,128)}, f32[3,96,768]{1,0,2:T(4,128)}, f32[3,96,768]{1,0,2:T(4,128)}, f32[3,96,768]{1,0,2:T(4,128)}, ...) | async-done | bytes 6660496
  805.6 3.2 copy.97
  (189 shorter events, 47.7 us)
Async XLA Ops:
  7.2 46.7 %all-gather.6.cloned.1.call-start = ((), (), s32[]{:S(2)}) async-start(), calls=%async_computation.5 | async-start | bytes 2654208 | tf_op jit(solution)/shard_map/all_gather | solution.py:70
  9.9 11.2 %copy-start.12 = (bf16[256,512]{1,0:T(8,128)(2,1)}, bf16[256,512]{1,0:T(8,128)(2,1)S(1)}, u32[]{:S(2)}) copy-start(bf16[256,512]{1,0:T(8,128)(2,1)S(1)} %rev.3) | copy-start | bytes 786436
  10.2 43.7 %copy-start.5 = (bf16[5,3,96,768]{3,2,1,0:T(8,128)(2,1)S(1)}, bf16[5,3,96,768]{3,2,1,0:T(8,128)(2,1)}, u32[]{:S(2)}) copy-start(bf16[5,3,96,768]{3,2,1,0:T(8,128)(2,1)} %param.9) | copy-start | bytes 6635524
  10.2 10.0 %copy-start.10 = (bf16[1,256,512]{2,1,0:T(8,128)(2,1)}, bf16[1,256,512]{2,1,0:T(8,128)(2,1)S(1)}, u32[]{:S(2)}) copy-start(bf16[1,256,512]{2,1,0:T(8,128)(2,1)S(1)} %compare_convert_fusion.1) | copy-start | bytes 786436
  10.6 45.5 %copy-start.14 = (f32[2,96,256]{2,1,0:T(8,128)}, f32[2,96,256]{2,1,0:T(8,128)S(1)}, u32[]{:S(2)}) copy-start(f32[2,96,256]{2,1,0:T(8,128)S(1)} %get-tuple-element.96) | copy-start | bytes 589828
  10.7 5.8 collective-permute-start
  15.2 5.0 collective-permute-start.1
  21.1 74.3 %all-gather.8.cloned.1.call-start = ((), (), s32[]{:S(2)}) async-start(), calls=%async_computation.6 | async-start | bytes 2654208 | tf_op jit(solution)/shard_map/all_gather | solution.py:70
  56.1 4.5 collective-permute-start.2
  59.3 4.8 collective-permute-start.3
  65.0 72.7 %all-gather.10.cloned.1.call-start = ((), (), s32[]{:S(2)}) async-start(), calls=%async_computation.7 | async-start | bytes 2654208 | tf_op jit(solution)/shard_map/all_gather | solution.py:70
  97.7 5.0 collective-permute-start.4
  100.9 5.7 collective-permute-start.5
  107.4 75.4 %all-gather.12.cloned.1.call-start = ((), (), s32[]{:S(2)}) async-start(), calls=%async_computation.8 | async-start | bytes 2654208 | tf_op jit(solution)/shard_map/all_gather | solution.py:70
  139.9 6.0 collective-permute-start.6
  144.0 10.6 %collective-permute-start.7 = (bf16[2,96,256]{2,1,0:T(8,128)(2,1)S(1)}, bf16[2,96,256]{2,1,0:T(8,128)(2,1)S(1)}, u32[]{:S(2)}, u32[]{:S(2)}) collective-permute-start(bf16[2,96,256]{2,1,0:T(8,128)(2,1)S(1)} %get-tuple-element.101), channel_id=1, source_target_pairs={{16,0},{24,8},{32,16},{40,24},{48,32},{56,40},{64,48},{72,56},{80,... | collective-permute-start | bytes 294920 | tf_op jit(solution)/shard_map/ppermute | solution.py:26
  155.5 76.1 %all-gather.14.cloned.1.call-start = ((), (), s32[]{:S(2)}) async-start(), calls=%async_computation.9 | async-start | bytes 2654208 | tf_op jit(solution)/shard_map/all_gather | solution.py:70
  185.0 21.1 %copy-start.19 = (s32[512]{0:T(512)S(1)}, s32[512]{0:T(512)}, u32[]{:S(2)}) copy-start(s32[512]{0:T(512)} %param.12) | copy-start | bytes 6148
  185.0 9.1 %collective-permute-start.8 = (bf16[2,96,256]{2,1,0:T(8,128)(2,1)S(1)}, bf16[2,96,256]{2,1,0:T(8,128)(2,1)S(1)}, u32[]{:S(2)}, u32[]{:S(2)}) collective-permute-start(bf16[2,96,256]{2,1,0:T(8,128)(2,1)S(1)} %get-tuple-element.103), channel_id=1, source_target_pairs={{0,32},{8,40},{16,48},{24,56},{32,64},{40,72},{48,80},{56,88},{64,... | collective-permute-start | bytes 294920 | tf_op jit(solution)/shard_map/ppermute | solution.py:26
  192.4 10.3 %collective-permute-start.9 = (bf16[2,96,256]{2,1,0:T(8,128)(2,1)S(1)}, bf16[2,96,256]{2,1,0:T(8,128)(2,1)S(1)}, u32[]{:S(2)}, u32[]{:S(2)}) collective-permute-start(bf16[2,96,256]{2,1,0:T(8,128)(2,1)S(1)} %get-tuple-element.103), channel_id=1, source_target_pairs={{32,0},{40,8},{48,16},{56,24},{64,32},{72,40},{80,48},{88,56},{96,... | collective-permute-start | bytes 294920 | tf_op jit(solution)/shard_map/ppermute | solution.py:26
  202.8 6.3 copy-start.22
  203.6 157.6 %reduce-scatter.6.cloned.1.call-start = ((), (), s32[]{:S(2)}) async-start(), calls=%async_computation.10 | async-start | bytes 1769472 | tf_op jit(solution)/shard_map/reduce_scatter | solution.py:116
  208.7 103.0 %copy-start.23 = (f32[512]{0:T(512)S(1)}, f32[512]{0:T(512)}, u32[]{:S(2)}) copy-start(f32[512]{0:T(512)} %param.13) | copy-start | bytes 6148
  311.7 16.6 %copy-start.20 = (f32[512]{0:T(512)}, f32[512]{0:T(512)S(1)}, u32[]{:S(2)}) copy-start(f32[512]{0:T(512)S(1)} %psum.21) | copy-start | bytes 6148
  312.2 9.4 %collective-permute-start.10 = (bf16[2,96,256]{2,1,0:T(8,128)(2,1)S(1)}, bf16[2,96,256]{2,1,0:T(8,128)(2,1)S(1)}, u32[]{:S(2)}, u32[]{:S(2)}) collective-permute-start(bf16[2,96,256]{2,1,0:T(8,128)(2,1)S(1)} %fusion.101), channel_id=1, source_target_pairs={{32,0},{40,8},{48,16},{56,24},{64,32},{72,40},{80,48},{88,56},{96,... | collective-permute-start | bytes 294920 | tf_op jit(solution)/shard_map/ppermute | solution.py:26
  313.5 13.0 %collective-permute-start.11 = (bf16[2,96,256]{2,1,0:T(8,128)(2,1)S(1)}, bf16[2,96,256]{2,1,0:T(8,128)(2,1)S(1)}, u32[]{:S(2)}, u32[]{:S(2)}) collective-permute-start(bf16[2,96,256]{2,1,0:T(8,128)(2,1)S(1)} %fusion.101), channel_id=1, source_target_pairs={{0,32},{8,40},{16,48},{24,56},{32,64},{40,72},{48,80},{56,88},{64,... | collective-permute-start | bytes 294920 | tf_op jit(solution)/shard_map/ppermute | solution.py:26
  328.3 83.5 %reduce-scatter.8.cloned.1.call-start = ((), (), s32[]{:S(2)}) async-start(), calls=%async_computation.11 | async-start | bytes 1769472 | tf_op jit(solution)/shard_map/reduce_scatter | solution.py:116
  362.3 9.7 %copy-start.6 = (bf16[2,96,256]{2,1,0:T(8,128)(2,1)}, bf16[2,96,256]{2,1,0:T(8,128)(2,1)S(1)}, u32[]{:S(2)}) copy-start(bf16[2,96,256]{2,1,0:T(8,128)(2,1)S(1)} %get-tuple-element.33) | copy-start | bytes 294916
  362.3 7.3 collective-permute-start.12
  363.6 6.5 collective-permute-start.13
  371.9 87.4 %reduce-scatter.10.cloned.1.call-start = ((), (), s32[]{:S(2)}) async-start(), calls=%async_computation.12 | async-start | bytes 1769472 | tf_op jit(solution)/shard_map/reduce_scatter | solution.py:116
  412.9 8.8 %copy-start.8 = (bf16[2,96,256]{2,1,0:T(8,128)(2,1)}, bf16[2,96,256]{2,1,0:T(8,128)(2,1)S(1)}, u32[]{:S(2)}) copy-start(bf16[2,96,256]{2,1,0:T(8,128)(2,1)S(1)} %get-tuple-element.31) | copy-start | bytes 294916
  412.9 5.4 collective-permute-start.14
  414.2 5.6 collective-permute-start.15
  421.7 84.7 %reduce-scatter.12.cloned.1.call-start = ((), (), s32[]{:S(2)}) async-start(), calls=%async_computation.13 | async-start | bytes 1769472 | tf_op jit(solution)/shard_map/reduce_scatter | solution.py:116
  460.4 5.3 collective-permute-start.16
  461.7 5.2 collective-permute-start.17
  468.7 86.8 %reduce-scatter.14.cloned.1.call-start = ((), (), s32[]{:S(2)}) async-start(), calls=%async_computation.14 | async-start | bytes 1769472 | tf_op jit(solution)/shard_map/reduce_scatter | solution.py:116
  508.2 5.5 collective-permute-start.18
  509.5 5.2 collective-permute-start.19
  517.8 287.8 %all-reduce.8.cloned.1.call-start = ((), (), s32[]{:S(2)}) async-start(), calls=%async_computation.15 | async-start | bytes 21569536
  519.5 6.0 copy-start.7
  537.2 18.3 %copy-start.11 = (bf16[1,256,512]{2,1,0:T(8,128)(2,1)S(1)}, bf16[1,256,512]{2,1,0:T(8,128)(2,1)}, u32[]{:S(2)}) copy-start(bf16[1,256,512]{2,1,0:T(8,128)(2,1)} %copy-done.10) | copy-start | bytes 786436
  537.2 18.3 %copy-start.13 = (bf16[256,512]{1,0:T(8,128)(2,1)S(1)}, bf16[256,512]{1,0:T(8,128)(2,1)}, u32[]{:S(2)}) copy-start(bf16[256,512]{1,0:T(8,128)(2,1)} %copy-done.12) | copy-start | bytes 786436
  537.2 18.3 %copy-start.15 = (f32[2,96,256]{2,1,0:T(8,128)S(1)}, f32[2,96,256]{2,1,0:T(8,128)}, u32[]{:S(2)}) copy-start(f32[2,96,256]{2,1,0:T(8,128)} %copy-done.14) | copy-start | bytes 589828
  537.2 18.2 %copy-start.16 = (f32[2,96,256]{2,1,0:T(8,128)S(1)}, f32[2,96,256]{2,1,0:T(8,128)}, u32[]{:S(2)}) copy-start(f32[2,96,256]{2,1,0:T(8,128)} %get-tuple-element.28) | copy-start | bytes 589828
  805.6 8.1 copy-start.1
  805.6 7.4 copy-start.18
  (8 other events, 21.6 us)
Sparse Core Ops, SparseCore 0:
  21.3 32.5 all-gather.5
  65.1 30.3 all-gather.7
  107.5 30.0 all-gather.9
  155.6 27.1 all-gather.11
  203.7 27.8 all-gather.13
  328.4 32.7 reduce-scatter.5
  372.0 39.7 reduce-scatter.7
  421.8 37.4 reduce-scatter.9
  468.8 37.5 reduce-scatter.11
  517.9 37.4 reduce-scatter.13
  560.7 244.8 all-reduce.7
where the time goes:
time: 822 us; the launch traced here: 820 us
  waiting for transfers between devices  594 us (72%)
  blocking collectives  76.7 us (9%)
  starting transfers between devices  60.7 us (7%)
  matrix products  32.7 us (4%)
  local copies, waits for them, and re-layouts  26.2 us (3%)
  between operations  15.4 us (2%)
  other arithmetic  14 us (2%)
    unnamed x12, waiting for transfers between devices  247 us
    reduce_scatter x5, waiting for transfers between devices, shards(): through = lax.psum_scatter(spread, 'ch', scatter_dimension=1, tiled=True)  165 us
    all_gather x5, waiting for transfers between devices, shards(): collected_taps = lax.all_gather(resident_taps, 'ch', axis=2, tiled=True)  143 us
    psum x1, blocking collectives, shards(): window_score = lax.psum(partial_score, ('seq', 'ch'))  76.7 us
    ppermute x12, starting transfers between devices, passed_along(): return lax.ppermute(value, axis, pairs)  39.3 us
    ppermute x12, waiting for transfers between devices, passed_along(): return lax.ppermute(value, axis, pairs)  30.9 us
  transfers between devices with their start and end apart: 31, of which 26 were waited for; matrix products, arithmetic and copies ran while one was open for 3% of the time, Pallas kernels for 0%

commit v1 on v0

--- a/solution.py
+++ b/solution.py
@@ -67,7 +67,14 @@
         active = jax.nn.gelu(residual_state).astype(jnp.bfloat16)
         lower_rows, upper_rows = reach_rows(active, spans[current_layer_index])
         resident_taps = order_taps(lower_rows, active, upper_rows)
-        collected_taps = lax.all_gather(resident_taps, "ch", axis=2, tiled=True)
+        ring = [resident_taps]
+        for hop in range(7):
+            ring.append(lax.ppermute(ring[-1], "ch", [(dev, (dev + 1) % 8) for dev in range(8)]))
+        collected_taps = jnp.roll(
+            jnp.concatenate(ring[::-1], axis=2),
+            (lax.axis_index("ch") + 1) * ring[0].shape[2],
+            axis=2,
+        )
         saved_states.append(residual_state)
         stored_taps.append(collected_taps)
         residual_state = residual_state + jnp.einsum(

time: 822 us -> 934 us (1.14)
  waiting for transfers between devices: 594 us -> 675 us
  starting transfers between devices: 60.7 us -> 80.6 us
  matrix products: 32.7 us -> 42.3 us
    ppermute x0 -> x35, waiting for transfers between devices: none -> 241 us  [shards(): lax.ppermute(ring[-1], 'ch', [(dev, (dev + 1) % 8) for dev in range(8)])]
    all_gather x5 -> x0, waiting for transfers between devices: 143 us -> none  [shards(): collected_taps = lax.all_gather(resident_taps, 'ch', axis=2, tiled=True)]
    ppermute x0 -> x35, starting transfers between devices: none -> 15 us  [shards(): lax.ppermute(ring[-1], 'ch', [(dev, (dev + 1) % 8) for dev in range(8)])]
    dot_general x5, matrix products: 7.84 us -> 18.3 us  [shards(): jnp.einsum('pygj,pij->yig', stored_taps[current_layer_index], incoming_gr...]
    unnamed x12 -> x7, waiting for transfers between devices: 247 us -> 246 us
  transfers between devices with their start and end apart: 31 -> 61, of which waited for: 26 -> 56; matrix products, arithmetic and copies ran while one was open for 3% -> 4% of each run, Pallas kernels for 0% -> 0%
where the time goes in v1:
time: 934 us; the launch traced here: 932 us
  waiting for transfers between devices  675 us (72%)
  blocking collectives  82.8 us (9%)
  starting transfers between devices  80.6 us (9%)
  matrix products  42.3 us (5%)
  local copies, waits for them, and re-layouts  25.7 us (3%)
  between operations  16.3 us (2%)
  other arithmetic  9.43 us (1%)
    unnamed x7, waiting for transfers between devices  246 us
    ppermute x35, waiting for transfers between devices, shards(): lax.ppermute(ring[-1], 'ch', [(dev, (dev + 1) % 8) for dev in range(8)])  241 us
    reduce_scatter x5, waiting for transfers between devices, shards(): through = lax.psum_scatter(spread, 'ch', scatter_dimension=1, tiled=True)  158 us
    psum x1, blocking collectives, shards(): window_score = lax.psum(partial_score, ('seq', 'ch'))  82.8 us
    ppermute x12, starting transfers between devices, passed_along(): return lax.ppermute(value, axis, pairs)  43.2 us
    ppermute x12, waiting for transfers between devices, passed_along(): return lax.ppermute(value, axis, pairs)  23 us
  transfers between devices with their start and end apart: 61, of which 56 were waited for; matrix products, arithmetic and copies ran while one was open for 4% of the time, Pallas kernels for 0%

profile of v1, /device:TPU:1, one launch (start us, length us, event | category | flops | bytes accessed | tf_op | source)
XLA Modules:
  0.0 932.2 jit_solution(16346334550598194519)
XLA Ops:
  10.7 4.4 collective-permute-start
  47.9 4.8 collective-permute-done.6
  54.1 6.0 collective-permute-done.7
  60.2 7.2 collective-permute-done.8
  76.6 8.3 collective-permute-done.11
  84.9 7.4 collective-permute-done.12
  92.3 7.4 collective-permute-done.13
  99.6 7.4 collective-permute-done.14
  107.0 7.4 collective-permute-done.15
  114.4 7.4 collective-permute-done.16
  121.7 7.4 collective-permute-done.17
  131.5 4.6 collective-permute-start.18
  137.7 5.2 collective-permute-done.19
  143.0 8.5 collective-permute-done.20
  151.5 7.4 collective-permute-done.21
  158.9 7.4 collective-permute-done.22
  166.2 7.4 collective-permute-done.23
  173.6 7.4 collective-permute-done.24
  181.0 7.4 collective-permute-done.25
  188.3 7.4 collective-permute-done.26
  198.1 7.8 collective-permute-start.27
  207.6 4.6 collective-permute-done.28
  212.5 8.6 collective-permute-done.29
  221.1 7.4 collective-permute-done.30
  228.5 7.4 collective-permute-done.31
  235.8 7.4 collective-permute-done.32
  243.2 7.4 collective-permute-done.33
  250.5 7.4 collective-permute-done.34
  257.9 7.4 collective-permute-done.35
  268.3 6.1 collective-permute-start.36
  276.0 7.6 collective-permute-done.37
  284.0 8.6 collective-permute-done.38
  292.6 7.4 collective-permute-done.39
  300.0 7.4 collective-permute-done.40
  308.5 6.2 collective-permute-done.41
  316.2 6.0 collective-permute-done.42
  322.4 7.3 collective-permute-done.43
  329.8 7.3 collective-permute-done.44
  342.6 82.8 %psum.21 = f32[512]{0:T(512)S(1)} all-reduce(f32[512]{0:T(512)S(1)} %broadcast_multiply_fusion), channel_id=1, replica_groups=mesh['seq'=32,'ch'=8] {'seq','ch'}, use_global_device_ids=true, to_apply=%region_1.3 | all-reduce | flops 512 | bytes 4096 | tf_op jit(solution)/shard_map/psum | solution.py:96
  427.2 7.9 collective-permute-start.46
  438.6 36.0 %reduce-scatter.6.cloned.1.call-done = f32[2,96,256]{2,1,0:T(8,128)} async-done(((f32[2,768,256]{2,1,0:T(8,128)}), f32[2,96,256]{2,1,0:T(8,128)}) %reduce-scatter.6.cloned.1.call-update) | async-done | bytes 196624 | tf_op jit(solution)/shard_map/reduce_scatter | solution.py:123
  477.0 4.9 collective-permute-start.48
  485.4 39.8 %reduce-scatter.8.cloned.1.call-done = f32[2,96,256]{2,1,0:T(8,128)} async-done(((f32[2,768,256]{2,1,0:T(8,128)}), f32[2,96,256]{2,1,0:T(8,128)}) %reduce-scatter.8.cloned.1.call-update) | async-done | bytes 196624 | tf_op jit(solution)/shard_map/reduce_scatter | solution.py:123
  535.0 37.7 %reduce-scatter.10.cloned.1.call-done = f32[2,96,256]{2,1,0:T(8,128)} async-done(((f32[2,768,256]{2,1,0:T(8,128)}), f32[2,96,256]{2,1,0:T(8,128)}) %reduce-scatter.10.cloned.1.call-update) | async-done | bytes 196624 | tf_op jit(solution)/shard_map/reduce_scatter | solution.py:123
  582.3 37.6 %reduce-scatter.12.cloned.1.call-done = f32[2,96,256]{2,1,0:T(8,128)} async-done(((f32[2,768,256]{2,1,0:T(8,128)}), f32[2,96,256]{2,1,0:T(8,128)}) %reduce-scatter.12.cloned.1.call-update) | async-done | bytes 196624 | tf_op jit(solution)/shard_map/reduce_scatter | solution.py:123
  622.5 4.2 collective-permute-start.54
  659.9 7.4 reduce-scatter.14.cloned.1.call-done
  671.1 246.1 %all-reduce.8.cloned.1.call-done = (f32[3,96,768]{1,0,2:T(4,128)}, f32[3,96,768]{1,0,2:T(4,128)}, f32[3,96,768]{1,0,2:T(4,128)}, f32[3,96,768]{1,0,2:T(4,128)}, ...) async-done(((f32[3,96,768]{1,0,2:T(4,128)}, f32[3,96,768]{1,0,2:T(4,128)}, f32[3,96,768]{1,0,2:T(4,128)}, f32[3,96,768]{1,0,2:T(4,128)}, ...) | async-done | bytes 6660496
  (312 shorter events, 145.2 us)
Async XLA Ops:
  7.2 467.4 %reduce-scatter.6.cloned.1.call-start = ((), (), s32[]{:S(2)}) async-start(), calls=%async_computation.5 | async-start | bytes 1769472 | tf_op jit(solution)/shard_map/reduce_scatter | solution.py:123
  20.3 6.7 collective-permute-start.2
  45.4 7.3 collective-permute-start.6
  52.7 7.4 collective-permute-start.7
  60.1 7.4 collective-permute-start.8
  76.6 8.3 collective-permute-start.11
  84.9 7.4 collective-permute-start.12
  92.3 7.4 collective-permute-start.13
  99.6 7.4 collective-permute-start.14
  107.0 7.4 collective-permute-start.15
  114.4 7.4 collective-permute-start.16
  121.7 7.4 collective-permute-start.17
  131.5 6.2 collective-permute-start.18
  136.1 6.8 collective-permute-start.19
  143.0 8.5 collective-permute-start.20
  151.5 7.4 collective-permute-start.21
  158.9 7.4 collective-permute-start.22
  166.2 7.4 collective-permute-start.23
  173.6 7.4 collective-permute-start.24
  181.0 7.4 collective-permute-start.25
  188.3 7.4 collective-permute-start.26
  198.1 9.5 %collective-permute-start.27 = (bf16[2,96,256]{2,1,0:T(8,128)(2,1)S(1)}, bf16[2,96,256]{2,1,0:T(8,128)(2,1)S(1)}, u32[]{:S(2)}, u32[]{:S(2)}) collective-permute-start(bf16[2,96,256]{2,1,0:T(8,128)(2,1)S(1)} %get-tuple-element.102), channel_id=1, source_target_pairs={{0,16},{8,24},{16,32},{24,40},{32,48},{40,56},{48,64},{56,72},{64,... | collective-permute-start | bytes 294920 | tf_op jit(solution)/shard_map/ppermute | solution.py:26
  205.9 6.3 collective-permute-start.28
  212.3 8.8 collective-permute-start.29
  221.1 7.4 collective-permute-start.30
  228.5 7.4 collective-permute-start.31
  235.8 7.4 collective-permute-start.32
  243.2 7.4 collective-permute-start.33
  250.5 7.4 collective-permute-start.34
  257.9 7.4 collective-permute-start.35
  268.3 7.7 collective-permute-start.36
  274.4 9.3 collective-permute-start.37
  283.8 8.8 collective-permute-start.38
  292.6 7.4 collective-permute-start.39
  300.0 7.4 collective-permute-start.40
  307.3 7.4 collective-permute-start.41
  314.7 7.5 collective-permute-start.42
  322.2 7.5 collective-permute-start.43
  329.7 7.4 collective-permute-start.44
  425.9 9.3 %collective-permute-start.45 = (bf16[2,96,256]{2,1,0:T(8,128)(2,1)S(1)}, bf16[2,96,256]{2,1,0:T(8,128)(2,1)S(1)}, u32[]{:S(2)}, u32[]{:S(2)}) collective-permute-start(bf16[2,96,256]{2,1,0:T(8,128)(2,1)S(1)} %fusion.106), channel_id=1, source_target_pairs={{32,0},{40,8},{48,16},{56,24},{64,32},{72,40},{80,48},{88,56},{96,... | collective-permute-start | bytes 294920 | tf_op jit(solution)/shard_map/ppermute | solution.py:26
  427.2 9.5 %collective-permute-start.46 = (bf16[2,96,256]{2,1,0:T(8,128)(2,1)S(1)}, bf16[2,96,256]{2,1,0:T(8,128)(2,1)S(1)}, u32[]{:S(2)}, u32[]{:S(2)}) collective-permute-start(bf16[2,96,256]{2,1,0:T(8,128)(2,1)S(1)} %fusion.106), channel_id=1, source_target_pairs={{0,32},{8,40},{16,48},{24,56},{32,64},{40,72},{48,80},{56,88},{64,... | collective-permute-start | bytes 294920 | tf_op jit(solution)/shard_map/ppermute | solution.py:26
  438.6 86.6 %reduce-scatter.8.cloned.1.call-start = ((), (), s32[]{:S(2)}) async-start(), calls=%async_computation.6 | async-start | bytes 1769472 | tf_op jit(solution)/shard_map/reduce_scatter | solution.py:123
  475.7 7.3 collective-permute-start.47
  477.0 6.5 collective-permute-start.48
  485.3 87.4 %reduce-scatter.10.cloned.1.call-start = ((), (), s32[]{:S(2)}) async-start(), calls=%async_computation.7 | async-start | bytes 1769472 | tf_op jit(solution)/shard_map/reduce_scatter | solution.py:123
  535.0 84.9 %reduce-scatter.12.cloned.1.call-start = ((), (), s32[]{:S(2)}) async-start(), calls=%async_computation.8 | async-start | bytes 1769472 | tf_op jit(solution)/shard_map/reduce_scatter | solution.py:123
  582.3 85.0 %reduce-scatter.14.cloned.1.call-start = ((), (), s32[]{:S(2)}) async-start(), calls=%async_computation.9 | async-start | bytes 1769472 | tf_op jit(solution)/shard_map/reduce_scatter | solution.py:123
  629.6 287.7 %all-reduce.8.cloned.1.call-start = ((), (), s32[]{:S(2)}) async-start(), calls=%async_computation.10 | async-start | bytes 21569536
  (52 other events, 1023.8 us)
Sparse Core Ops, SparseCore 0:
  438.7 35.8 reduce-scatter.5
  485.4 39.6 reduce-scatter.7
  535.1 37.5 reduce-scatter.9
  582.4 37.4 reduce-scatter.11
  629.7 37.5 reduce-scatter.13
  672.4 244.7 all-reduce.7
